TPU v7x, 256 devices: a whole 4x4x8 slice. The times are simulated.
256 devices in a mesh: pool: 4 (over x_hi, core), frame: 16 (over x_lo, z), tensor: 4 (over y).
Axes of the slice: x: 4 (x_hi: 2, x_lo: 2; x = x_hi * 2 + x_lo), y: 4, z: 8, core: 2. Of those that a mesh axis runs over, the one named last changes fastest.
Arguments:
- latents: bfloat16 [32768, 2240], P(('pool', 'frame', 'tensor')), parts along dimension 0, may hold values from -6 to 6
- queries: bfloat16 [32768, 2240], P(('pool', 'frame'), 'tensor'), parts along dimension 0, may hold values from -6 to 6
- keys: bfloat16 [32768, 2240], P(('pool', 'frame'), 'tensor'), parts along dimension 0, may hold values from -6 to 6
- values: bfloat16 [32768, 2240], P(('pool', 'frame'), 'tensor'), parts along dimension 0, may hold values from -6 to 6
- log_decay: float32 [20, 32768], P('tensor', ('pool', 'frame')), parts along dimension 1, may hold values from -0.6 to 0, as said below
- block_ids: int32 [32768], P(('pool', 'frame')), parts along dimension 0, may hold values from 0 to 3, as said below
- t_index: int32 [4], P('pool'), parts along dimension 0, may hold values from 0 to 49
- w_mod: bfloat16 [256, 8960], replicated, may hold values from -0.375 to 0.375
- w_out: bfloat16 [2240, 2240], P('tensor', 'frame'), may hold values from -0.125 to 0.125
- w_up: bfloat16 [2240, 4480], P('frame', 'tensor'), may hold values from -0.125 to 0.125
- w_down: bfloat16 [4480, 2240], P('tensor', 'frame'), may hold values from -0.09375 to 0.09375
Outputs:
- velocity: bfloat16 [32768, 2240], P(('pool', 'frame', 'tensor')), parts along dimension 0
- advanced: bfloat16 [32768, 2240], P(('pool', 'frame', 'tensor')), parts along dimension 0
There are 4 independent parts, one for each index of `pool`. A program takes and returns all parts, laid end to end along the dimension named above; an argument that names none is the same for every part. Nothing has to cross between parts.
Inputs may be any that keep to these rules, and one draw needn't show every extreme that they name: `block_ids`: within each span of 512 tokens the value never falls, starts at 0 and ends at 3. `log_decay`: every entry is negative.
All inputs are finite; a program needn't handle non-finite values.
Results may differ from a plain program's by a relative error of at most 0.0085.
Values may be sent and summed in bfloat16 or wider, within the bound.
No kernel may reach another device: no remote copies, remote signals or barrier semaphores. Data moves between devices by JAX's collectives and lax.ppermute only.
A program may use at most 128 MiB of HBM per device.

v0:
```python
import math
import jax
import jax.numpy as jnp
from jax import lax
from jax.sharding import PartitionSpec as P

STEPS = 50


def shifted(block, axis, distance):
    devices = range(lax.axis_size(axis))
    route = [(i - distance, i) for i in devices if i - distance in devices]
    return lax.ppermute(block, axis, route)


def modulation_of(t_index, w_mod):
    fraction = 1.0 - t_index[0].astype(jnp.float32) / STEPS
    following = fraction - 1.0 / STEPS
    sigma_now = 3.0 * fraction / (1.0 + 2.0 * fraction)
    sigma_next = 3.0 * following / (1.0 + 2.0 * following)
    half_width = w_mod.shape[0] // 2
    frequency = jnp.exp(
        -math.log(10000.0) * jnp.arange(half_width).astype(jnp.float32) / half_width
    )
    angles = 1000.0 * sigma_now * frequency
    embedding = jnp.concatenate([jnp.cos(angles), jnp.sin(angles)])
    time_features = jax.nn.silu(embedding).astype(jnp.bfloat16)
    shifts = jnp.dot(time_features[None, :], w_mod, preferred_element_type=jnp.float32)[0]
    return (shifts, sigma_next - sigma_now)


def own_state(key_heads, value_heads, cumulative):
    block_total = cumulative[:, -1]
    scaled = key_heads.astype(jnp.float32) * jnp.exp(block_total[:, None] - cumulative)[:, :, None]
    state_sum = jnp.einsum(
        "htd,hte->hde", scaled, value_heads.astype(jnp.float32), precision=lax.Precision.HIGHEST
    )
    return (block_total, state_sum)


def mix_block(query_heads, key_heads, value_heads, cumulative, labels, carried_state):
    factor = query_heads.shape[2] ** (-0.5)
    visible = labels[None, :] <= labels[:, None]
    decay = jnp.exp(jnp.minimum(cumulative[:, :, None] - cumulative[:, None, :], 0.0))
    weights = jnp.where(visible[None], decay, 0.0) * factor
    scores = jnp.einsum("hid,hjd->hij", query_heads, key_heads, preferred_element_type=jnp.float32)
    probs = (scores * weights).astype(jnp.bfloat16)
    inner_part = jnp.einsum("hij,hjd->hid", probs, value_heads, preferred_element_type=jnp.float32)
    carried = jnp.einsum(
        "hid,hde->hie",
        query_heads.astype(jnp.float32),
        carried_state,
        precision=lax.Precision.HIGHEST,
    )
    numerator = inner_part + carried * (jnp.exp(cumulative) * factor)[:, :, None]
    normed = numerator * lax.rsqrt(jnp.mean(numerator * numerator, axis=2, keepdims=True) + 1e-06)
    return normed.astype(jnp.bfloat16)


def layer_norm(hidden):
    centered = hidden - jnp.mean(hidden, axis=1, keepdims=True)
    variance = jnp.mean(centered * centered, axis=1, keepdims=True)
    return centered * lax.rsqrt(variance + 1e-06)


def on_device(
    latents, queries, keys, values, log_decay, block_ids, t_index, w_mod, w_out, w_up, w_down
):
    shifts, step_size = modulation_of(t_index, w_mod)
    width = latents.shape[1]
    head_count = log_decay.shape[0]
    token_count = log_decay.shape[1]
    head_size = queries.shape[1] // head_count

    def to_heads(rows_in):
        return rows_in.reshape(token_count, head_count, head_size).transpose(1, 0, 2)

    query_heads = to_heads(queries)
    key_heads = to_heads(keys)
    value_heads = to_heads(values)
    cumulative = jnp.cumsum(log_decay, axis=1)
    block_total, state_sum = own_state(key_heads, value_heads, cumulative)
    keep_factor = jnp.exp(block_total)[:, None, None]

    def relay(turn, incoming):
        return shifted(
            (keep_factor * incoming + state_sum).astype(jnp.bfloat16), "frame", 1
        ).astype(jnp.float32)

    carried_state = lax.fori_loop(0, lax.axis_size("frame") - 1, relay, jnp.zeros_like(state_sum))
    mixed = mix_block(query_heads, key_heads, value_heads, cumulative, block_ids, carried_state)
    mixed_rows = mixed.transpose(1, 0, 2).reshape(token_count, head_count * head_size)
    head_terms = jnp.dot(
        mixed_rows,
        lax.all_gather(w_out, "frame", axis=1, tiled=True),
        preferred_element_type=jnp.float32,
    )
    attention = lax.psum_scatter(
        head_terms.astype(jnp.bfloat16), "tensor", scatter_dimension=0, tiled=True
    ).astype(jnp.float32)
    hidden = latents.astype(jnp.float32) + shifts[3 * width :] * attention
    normed = (layer_norm(hidden) * (1.0 + shifts[width : 2 * width]) + shifts[:width]).astype(
        jnp.bfloat16
    )
    normed_all = lax.all_gather(normed, "tensor", axis=0, tiled=True)
    up_sums = jnp.dot(
        normed_all,
        lax.all_gather(w_up, "frame", axis=0, tiled=True),
        preferred_element_type=jnp.float32,
    )
    units = jax.nn.gelu(up_sums, approximate=True).astype(jnp.bfloat16)
    unit_terms = jnp.dot(
        units,
        lax.all_gather(w_down, "frame", axis=1, tiled=True),
        preferred_element_type=jnp.float32,
    )
    feed = lax.psum_scatter(
        unit_terms.astype(jnp.bfloat16), "tensor", scatter_dimension=0, tiled=True
    ).astype(jnp.float32)
    velocity = (hidden + shifts[2 * width : 3 * width] * feed).astype(jnp.bfloat16)
    advanced = (latents.astype(jnp.float32) + step_size * velocity.astype(jnp.float32)).astype(
        jnp.bfloat16
    )
    return (velocity, advanced)


def solution(mesh):
    return jax.shard_map(
        on_device,
        mesh=mesh,
        in_specs=(
            P(("pool", "frame", "tensor"), None),
            P(("pool", "frame"), "tensor"),
            P(("pool", "frame"), "tensor"),
            P(("pool", "frame"), "tensor"),
            P("tensor", ("pool", "frame")),
            P(("pool", "frame")),
            P("pool"),
            P(),
            P("tensor", "frame"),
            P("frame", "tensor"),
            P("tensor", "frame"),
        ),
        out_specs=(P(("pool", "frame", "tensor"), None), P(("pool", "frame", "tensor"), None)),
        check_vma=False,
    )
```

profile of v0, /device:TPU:1, one launch (start us, length us, event | category | flops | bytes accessed | tf_op | source)
XLA Modules:
  0.0 474.8 jit_solution(17253476656250877932)
XLA Ops:
  13.8 120.2 %while.11 = (s32[]{:T(128)}, f32[5,112,112]{2,1,0:T(8,128)S(1)}, f32[5,1,1]{0,2,1:T(1,128)S(1)}, f32[5,112,112]{2,1,0:T(8,128)S(1)}, s32[]{:T(128)}, /*index=5*/s32[]{:T(128)}) while((s32[]{:T(128)}, f32[5,112,112]{2,1,0:T(8,128)S(1)}, f32[5,1,1]{0,2,1:T(1,128)S(1)}, f32[5,112,112]{2,1,0:T(8,128)S(1)}, s32[]{:T(128)}, ...), condition=%wide.region_3.4_spmd.clone, body=%wide.region_2.3_spmd.clone.sunk | while | flops 313603 | bytes 1505419 | solution.py:90
  13.9 4.4 collective-permute-start
  20.9 4.1 collective-permute-start
  25.0 3.9 collective-permute-done
  29.1 5.2 %collective-permute-start = (bf16[5,112,112]{2,1,0:T(8,128)(2,1)S(1)}, bf16[5,112,112]{2,1,0:T(8,128)(2,1)S(1)}, u32[]{:S(2)}, u32[]{:S(2)}) collective-permute-start(bf16[5,112,112]{2,1,0:T(8,128)(2,1)S(1)} %fusion.58), channel_id=1, source_target_pairs={{0,4},{4,8},{8,12},{12,16},{16,20},{20,24},{24,28},{28,32},{32,36}... | collective-permute-start | bytes 376328 | tf_op jit(solution)/shard_map/while/body/eval_jaxpr/ppermute | solution.py:13
  34.2 4.6 collective-permute-done
  39.0 4.1 collective-permute-start
  43.1 4.7 collective-permute-done
  48.0 4.1 collective-permute-start
  55.8 4.4 collective-permute-start
  63.9 5.8 %collective-permute-start = (bf16[5,112,112]{2,1,0:T(8,128)(2,1)S(1)}, bf16[5,112,112]{2,1,0:T(8,128)(2,1)S(1)}, u32[]{:S(2)}, u32[]{:S(2)}) collective-permute-start(bf16[5,112,112]{2,1,0:T(8,128)(2,1)S(1)} %fusion.58), channel_id=1, source_target_pairs={{0,4},{4,8},{8,12},{12,16},{16,20},{20,24},{24,28},{28,32},{32,36}... | collective-permute-start | bytes 376328 | tf_op jit(solution)/shard_map/while/body/eval_jaxpr/ppermute | solution.py:13
  69.7 3.8 collective-permute-done
  73.6 5.2 %collective-permute-start = (bf16[5,112,112]{2,1,0:T(8,128)(2,1)S(1)}, bf16[5,112,112]{2,1,0:T(8,128)(2,1)S(1)}, u32[]{:S(2)}, u32[]{:S(2)}) collective-permute-start(bf16[5,112,112]{2,1,0:T(8,128)(2,1)S(1)} %fusion.58), channel_id=1, source_target_pairs={{0,4},{4,8},{8,12},{12,16},{16,20},{20,24},{24,28},{28,32},{32,36}... | collective-permute-start | bytes 376328 | tf_op jit(solution)/shard_map/while/body/eval_jaxpr/ppermute | solution.py:13
  81.2 5.2 %collective-permute-start = (bf16[5,112,112]{2,1,0:T(8,128)(2,1)S(1)}, bf16[5,112,112]{2,1,0:T(8,128)(2,1)S(1)}, u32[]{:S(2)}, u32[]{:S(2)}) collective-permute-start(bf16[5,112,112]{2,1,0:T(8,128)(2,1)S(1)} %fusion.58), channel_id=1, source_target_pairs={{0,4},{4,8},{8,12},{12,16},{16,20},{20,24},{24,28},{28,32},{32,36}... | collective-permute-start | bytes 376328 | tf_op jit(solution)/shard_map/while/body/eval_jaxpr/ppermute | solution.py:13
  88.6 4.4 collective-permute-start
  95.2 5.6 %collective-permute-start = (bf16[5,112,112]{2,1,0:T(8,128)(2,1)S(1)}, bf16[5,112,112]{2,1,0:T(8,128)(2,1)S(1)}, u32[]{:S(2)}, u32[]{:S(2)}) collective-permute-start(bf16[5,112,112]{2,1,0:T(8,128)(2,1)S(1)} %fusion.58), channel_id=1, source_target_pairs={{0,4},{4,8},{8,12},{12,16},{16,20},{20,24},{24,28},{28,32},{32,36}... | collective-permute-start | bytes 376328 | tf_op jit(solution)/shard_map/while/body/eval_jaxpr/ppermute | solution.py:13
  103.0 5.1 %collective-permute-start = (bf16[5,112,112]{2,1,0:T(8,128)(2,1)S(1)}, bf16[5,112,112]{2,1,0:T(8,128)(2,1)S(1)}, u32[]{:S(2)}, u32[]{:S(2)}) collective-permute-start(bf16[5,112,112]{2,1,0:T(8,128)(2,1)S(1)} %fusion.58), channel_id=1, source_target_pairs={{0,4},{4,8},{8,12},{12,16},{16,20},{20,24},{24,28},{28,32},{32,36}... | collective-permute-start | bytes 376328 | tf_op jit(solution)/shard_map/while/body/eval_jaxpr/ppermute | solution.py:13
  111.1 5.6 %collective-permute-start = (bf16[5,112,112]{2,1,0:T(8,128)(2,1)S(1)}, bf16[5,112,112]{2,1,0:T(8,128)(2,1)S(1)}, u32[]{:S(2)}, u32[]{:S(2)}) collective-permute-start(bf16[5,112,112]{2,1,0:T(8,128)(2,1)S(1)} %fusion.58), channel_id=1, source_target_pairs={{0,4},{4,8},{8,12},{12,16},{16,20},{20,24},{24,28},{28,32},{32,36}... | collective-permute-start | bytes 376328 | tf_op jit(solution)/shard_map/while/body/eval_jaxpr/ppermute | solution.py:13
  119.9 5.4 %collective-permute-start = (bf16[5,112,112]{2,1,0:T(8,128)(2,1)S(1)}, bf16[5,112,112]{2,1,0:T(8,128)(2,1)S(1)}, u32[]{:S(2)}, u32[]{:S(2)}) collective-permute-start(bf16[5,112,112]{2,1,0:T(8,128)(2,1)S(1)} %fusion.58), channel_id=1, source_target_pairs={{0,4},{4,8},{8,12},{12,16},{16,20},{20,24},{24,28},{28,32},{32,36}... | collective-permute-start | bytes 376328 | tf_op jit(solution)/shard_map/while/body/eval_jaxpr/ppermute | solution.py:13
  127.5 4.4 collective-permute-start
  134.7 3.9 fusion.17
  142.9 4.4 convolution_convert_fusion.1
  147.3 4.2 copy.26
  156.8 60.6 %reduce-scatter.7.cloned.1.call-done = bf16[128,2240]{1,0:T(8,128)(2,1)} async-done(((bf16[512,2240]{1,0:T(8,128)(2,1)}), bf16[128,2240]{1,0:T(8,128)(2,1)}) %reduce-scatter.7.cloned.1.call-update) | async-done | bytes 573456
  222.0 66.8 %all-gather.12.cloned.1.call-done = bf16[16,140,1120]{2,1,0:T(8,128)(2,1)} async-done(((bf16[1,140,1120]{2,1,0:T(8,128)(2,1)}), bf16[16,140,1120]{2,1,0:T(8,128)(2,1)}) %all-gather.12.cloned.1.call-update) | async-done | bytes 5017616 | tf_op jit(solution)/shard_map/all_gather | solution.py:108
  288.7 7.9 %reshape.185 = bf16[2240,1120]{1,0:T(8,128)(2,1)} reshape(bf16[16,140,1120]{2,1,0:T(8,128)(2,1)} %all-gather.12.cloned.1.call-done) | data formatting | bytes 10035200
  296.6 69.5 %all-gather.14.cloned.1.call-done = bf16[16,140,1120]{2,1,0:T(8,128)(2,1)} async-done(((bf16[1,140,1120]{2,1,0:T(8,128)(2,1)}), bf16[16,140,1120]{2,1,0:T(8,128)(2,1)}) %all-gather.14.cloned.1.call-update) | async-done | bytes 5017616 | tf_op jit(solution)/shard_map/all_gather | solution.py:114
  366.1 7.9 %reshape.187 = bf16[2240,1120]{1,0:T(8,128)(2,1)} reshape(bf16[16,140,1120]{2,1,0:T(8,128)(2,1)} %all-gather.14.cloned.1.call-done) | data formatting | bytes 10035200
  374.0 37.2 %all-gather.8.cloned.1.call-done = bf16[512,2240]{0,1:T(8,128)(2,1)} async-done(((bf16[128,2240]{0,1:T(8,128)(2,1)}), bf16[512,2240]{0,1:T(8,128)(2,1)}) %all-gather.8.cloned.1.call-update) | async-done | bytes 2293776 | tf_op jit(solution)/shard_map/all_gather | solution.py:105
  411.1 12.2 %convolution_convert_fusion = bf16[512,2240]{0,1:T(8,128)(2,1)} fusion(bf16[2240,1120]{1,0:T(8,128)(2,1)} %reshape.187, bf16[512,2240]{0,1:T(8,128)(2,1)} %all-gather.8.cloned.1.call-done, bf16[2240,1120]{1,0:T(8,128)(2,1)} %reshape.185), kind=kOutput, calls=%fused_computation.4 | convolution fusion | flops 5144330240 | bytes 14622720 | tf_op jit(solution)/shard_map/dot_general | solution.py:112
  423.3 4.2 copy.28
  427.7 36.8 %reduce-scatter.9.cloned.1.call-done = bf16[128,2240]{1,0:T(8,128)(2,1)} async-done(((bf16[512,2240]{1,0:T(8,128)(2,1)}), bf16[128,2240]{1,0:T(8,128)(2,1)}) %reduce-scatter.9.cloned.1.call-update) | async-done | bytes 573456
  (91 shorter events, 53.9 us)
Async XLA Ops:
  7.2 126.8 %copy-start = (bf16[512,560]{0,1:T(8,128)(2,1)S(1)}, bf16[512,560]{0,1:T(8,128)(2,1)}, u32[]{:S(2)}) copy-start(bf16[512,560]{0,1:T(8,128)(2,1)} %param.14) | copy-start | bytes 1720324
  7.2 132.5 %all-gather.10.cloned.1.call-start = ((), (), s32[]{:S(2)}) async-start(), calls=%async_computation.3 | async-start | bytes 3133440 | tf_op jit(solution)/shard_map/all_gather | solution.py:95
  7.9 209.5 %reduce-scatter.7.cloned.1.call-start = ((), (), s32[]{:S(2)}) async-start(), calls=%async_computation.6 | async-start | bytes 2949120
  13.9 6.8 %collective-permute-start = (bf16[5,112,112]{2,1,0:T(8,128)(2,1)S(1)}, bf16[5,112,112]{2,1,0:T(8,128)(2,1)S(1)}, u32[]{:S(2)}, u32[]{:S(2)}) collective-permute-start(bf16[5,112,112]{2,1,0:T(8,128)(2,1)S(1)} %fusion.58), channel_id=1, source_target_pairs={{0,4},{4,8},{8,12},{12,16},{16,20},{20,24},{24,28},{28,32},{32,36}... | collective-permute-start | bytes 376328 | tf_op jit(solution)/shard_map/while/body/eval_jaxpr/ppermute | solution.py:13
  20.9 8.0 %collective-permute-start = (bf16[5,112,112]{2,1,0:T(8,128)(2,1)S(1)}, bf16[5,112,112]{2,1,0:T(8,128)(2,1)S(1)}, u32[]{:S(2)}, u32[]{:S(2)}) collective-permute-start(bf16[5,112,112]{2,1,0:T(8,128)(2,1)S(1)} %fusion.58), channel_id=1, source_target_pairs={{0,4},{4,8},{8,12},{12,16},{16,20},{20,24},{24,28},{28,32},{32,36}... | collective-permute-start | bytes 376328 | tf_op jit(solution)/shard_map/while/body/eval_jaxpr/ppermute | solution.py:13
  29.1 9.8 %collective-permute-start = (bf16[5,112,112]{2,1,0:T(8,128)(2,1)S(1)}, bf16[5,112,112]{2,1,0:T(8,128)(2,1)S(1)}, u32[]{:S(2)}, u32[]{:S(2)}) collective-permute-start(bf16[5,112,112]{2,1,0:T(8,128)(2,1)S(1)} %fusion.58), channel_id=1, source_target_pairs={{0,4},{4,8},{8,12},{12,16},{16,20},{20,24},{24,28},{28,32},{32,36}... | collective-permute-start | bytes 376328 | tf_op jit(solution)/shard_map/while/body/eval_jaxpr/ppermute | solution.py:13
  39.0 8.9 %collective-permute-start = (bf16[5,112,112]{2,1,0:T(8,128)(2,1)S(1)}, bf16[5,112,112]{2,1,0:T(8,128)(2,1)S(1)}, u32[]{:S(2)}, u32[]{:S(2)}) collective-permute-start(bf16[5,112,112]{2,1,0:T(8,128)(2,1)S(1)} %fusion.58), channel_id=1, source_target_pairs={{0,4},{4,8},{8,12},{12,16},{16,20},{20,24},{24,28},{28,32},{32,36}... | collective-permute-start | bytes 376328 | tf_op jit(solution)/shard_map/while/body/eval_jaxpr/ppermute | solution.py:13
  48.0 7.7 %collective-permute-start = (bf16[5,112,112]{2,1,0:T(8,128)(2,1)S(1)}, bf16[5,112,112]{2,1,0:T(8,128)(2,1)S(1)}, u32[]{:S(2)}, u32[]{:S(2)}) collective-permute-start(bf16[5,112,112]{2,1,0:T(8,128)(2,1)S(1)} %fusion.58), channel_id=1, source_target_pairs={{0,4},{4,8},{8,12},{12,16},{16,20},{20,24},{24,28},{28,32},{32,36}... | collective-permute-start | bytes 376328 | tf_op jit(solution)/shard_map/while/body/eval_jaxpr/ppermute | solution.py:13
  55.8 7.9 %collective-permute-start = (bf16[5,112,112]{2,1,0:T(8,128)(2,1)S(1)}, bf16[5,112,112]{2,1,0:T(8,128)(2,1)S(1)}, u32[]{:S(2)}, u32[]{:S(2)}) collective-permute-start(bf16[5,112,112]{2,1,0:T(8,128)(2,1)S(1)} %fusion.58), channel_id=1, source_target_pairs={{0,4},{4,8},{8,12},{12,16},{16,20},{20,24},{24,28},{28,32},{32,36}... | collective-permute-start | bytes 376328 | tf_op jit(solution)/shard_map/while/body/eval_jaxpr/ppermute | solution.py:13
  63.9 9.6 %collective-permute-start = (bf16[5,112,112]{2,1,0:T(8,128)(2,1)S(1)}, bf16[5,112,112]{2,1,0:T(8,128)(2,1)S(1)}, u32[]{:S(2)}, u32[]{:S(2)}) collective-permute-start(bf16[5,112,112]{2,1,0:T(8,128)(2,1)S(1)} %fusion.58), channel_id=1, source_target_pairs={{0,4},{4,8},{8,12},{12,16},{16,20},{20,24},{24,28},{28,32},{32,36}... | collective-permute-start | bytes 376328 | tf_op jit(solution)/shard_map/while/body/eval_jaxpr/ppermute | solution.py:13
  73.6 7.4 %collective-permute-start = (bf16[5,112,112]{2,1,0:T(8,128)(2,1)S(1)}, bf16[5,112,112]{2,1,0:T(8,128)(2,1)S(1)}, u32[]{:S(2)}, u32[]{:S(2)}) collective-permute-start(bf16[5,112,112]{2,1,0:T(8,128)(2,1)S(1)} %fusion.58), channel_id=1, source_target_pairs={{0,4},{4,8},{8,12},{12,16},{16,20},{20,24},{24,28},{28,32},{32,36}... | collective-permute-start | bytes 376328 | tf_op jit(solution)/shard_map/while/body/eval_jaxpr/ppermute | solution.py:13
  81.2 7.2 %collective-permute-start = (bf16[5,112,112]{2,1,0:T(8,128)(2,1)S(1)}, bf16[5,112,112]{2,1,0:T(8,128)(2,1)S(1)}, u32[]{:S(2)}, u32[]{:S(2)}) collective-permute-start(bf16[5,112,112]{2,1,0:T(8,128)(2,1)S(1)} %fusion.58), channel_id=1, source_target_pairs={{0,4},{4,8},{8,12},{12,16},{16,20},{20,24},{24,28},{28,32},{32,36}... | collective-permute-start | bytes 376328 | tf_op jit(solution)/shard_map/while/body/eval_jaxpr/ppermute | solution.py:13
  88.6 6.4 %collective-permute-start = (bf16[5,112,112]{2,1,0:T(8,128)(2,1)S(1)}, bf16[5,112,112]{2,1,0:T(8,128)(2,1)S(1)}, u32[]{:S(2)}, u32[]{:S(2)}) collective-permute-start(bf16[5,112,112]{2,1,0:T(8,128)(2,1)S(1)} %fusion.58), channel_id=1, source_target_pairs={{0,4},{4,8},{8,12},{12,16},{16,20},{20,24},{24,28},{28,32},{32,36}... | collective-permute-start | bytes 376328 | tf_op jit(solution)/shard_map/while/body/eval_jaxpr/ppermute | solution.py:13
  95.2 7.7 %collective-permute-start = (bf16[5,112,112]{2,1,0:T(8,128)(2,1)S(1)}, bf16[5,112,112]{2,1,0:T(8,128)(2,1)S(1)}, u32[]{:S(2)}, u32[]{:S(2)}) collective-permute-start(bf16[5,112,112]{2,1,0:T(8,128)(2,1)S(1)} %fusion.58), channel_id=1, source_target_pairs={{0,4},{4,8},{8,12},{12,16},{16,20},{20,24},{24,28},{28,32},{32,36}... | collective-permute-start | bytes 376328 | tf_op jit(solution)/shard_map/while/body/eval_jaxpr/ppermute | solution.py:13
  103.0 8.0 %collective-permute-start = (bf16[5,112,112]{2,1,0:T(8,128)(2,1)S(1)}, bf16[5,112,112]{2,1,0:T(8,128)(2,1)S(1)}, u32[]{:S(2)}, u32[]{:S(2)}) collective-permute-start(bf16[5,112,112]{2,1,0:T(8,128)(2,1)S(1)} %fusion.58), channel_id=1, source_target_pairs={{0,4},{4,8},{8,12},{12,16},{16,20},{20,24},{24,28},{28,32},{32,36}... | collective-permute-start | bytes 376328 | tf_op jit(solution)/shard_map/while/body/eval_jaxpr/ppermute | solution.py:13
  111.1 8.7 %collective-permute-start = (bf16[5,112,112]{2,1,0:T(8,128)(2,1)S(1)}, bf16[5,112,112]{2,1,0:T(8,128)(2,1)S(1)}, u32[]{:S(2)}, u32[]{:S(2)}) collective-permute-start(bf16[5,112,112]{2,1,0:T(8,128)(2,1)S(1)} %fusion.58), channel_id=1, source_target_pairs={{0,4},{4,8},{8,12},{12,16},{16,20},{20,24},{24,28},{28,32},{32,36}... | collective-permute-start | bytes 376328 | tf_op jit(solution)/shard_map/while/body/eval_jaxpr/ppermute | solution.py:13
  119.9 7.4 %collective-permute-start = (bf16[5,112,112]{2,1,0:T(8,128)(2,1)S(1)}, bf16[5,112,112]{2,1,0:T(8,128)(2,1)S(1)}, u32[]{:S(2)}, u32[]{:S(2)}) collective-permute-start(bf16[5,112,112]{2,1,0:T(8,128)(2,1)S(1)} %fusion.58), channel_id=1, source_target_pairs={{0,4},{4,8},{8,12},{12,16},{16,20},{20,24},{24,28},{28,32},{32,36}... | collective-permute-start | bytes 376328 | tf_op jit(solution)/shard_map/while/body/eval_jaxpr/ppermute | solution.py:13
  127.5 6.5 %collective-permute-start = (bf16[5,112,112]{2,1,0:T(8,128)(2,1)S(1)}, bf16[5,112,112]{2,1,0:T(8,128)(2,1)S(1)}, u32[]{:S(2)}, u32[]{:S(2)}) collective-permute-start(bf16[5,112,112]{2,1,0:T(8,128)(2,1)S(1)} %fusion.58), channel_id=1, source_target_pairs={{0,4},{4,8},{8,12},{12,16},{16,20},{20,24},{24,28},{28,32},{32,36}... | collective-permute-start | bytes 376328 | tf_op jit(solution)/shard_map/while/body/eval_jaxpr/ppermute | solution.py:13
  151.5 137.2 %all-gather.12.cloned.1.call-start = ((), (), s32[]{:S(2)}) async-start(), calls=%async_computation.4 | async-start | bytes 5640192 | tf_op jit(solution)/shard_map/all_gather | solution.py:108
  152.3 213.8 %all-gather.14.cloned.1.call-start = ((), (), s32[]{:S(2)}) async-start(), calls=%async_computation.5 | async-start | bytes 5640192 | tf_op jit(solution)/shard_map/all_gather | solution.py:114
  152.8 258.3 %all-gather.8.cloned.1.call-start = ((), (), s32[]{:S(2)}) async-start(), calls=%async_computation.2 | async-start | bytes 2867200 | tf_op jit(solution)/shard_map/all_gather | solution.py:105
  156.7 62.1 %copy-start.1 = (bf16[128,2240]{0,1:T(8,128)(2,1)S(1)}, bf16[128,2240]{0,1:T(8,128)(2,1)}, u32[]{:S(2)}) copy-start(bf16[128,2240]{0,1:T(8,128)(2,1)} %param.13) | copy-start | bytes 1720324
  221.7 242.7 %reduce-scatter.9.cloned.1.call-start = ((), (), s32[]{:S(2)}) async-start(), calls=%async_computation.7 | async-start | bytes 2949120
Sparse Core Ops, SparseCore 0:
  9.8 66.7 all-gather.9
  151.6 65.7 reduce-scatter.6
  219.2 69.4 all-gather.11
  290.4 75.6 all-gather.13
  368.3 42.7 all-gather.7
  427.7 36.6 reduce-scatter.8
where the time goes:
time: 476 us; the launch traced here: 475 us
  waiting for transfers between devices  318 us (67%)
  starting transfers between devices  73.3 us (15%)
  local copies, waits for them, and re-layouts  31.4 us (7%)
  matrix products  26.2 us (6%)
  between operations  15 us (3%)
  other arithmetic  10.9 us (2%)
    unnamed x8, waiting for transfers between devices  99.3 us
    ppermute x15, starting transfers between devices, shifted(): return lax.ppermute(block, axis, route)  72.9 us
    all_gather x1, waiting for transfers between devices, on_device(): lax.all_gather(w_down, 'frame', axis=1, tiled=True)  69.5 us
    all_gather x1, waiting for transfers between devices, on_device(): lax.all_gather(w_up, 'frame', axis=0, tiled=True)  66.8 us
    ppermute x15, waiting for transfers between devices, shifted(): return lax.ppermute(block, axis, route)  45 us
    all_gather x1, waiting for transfers between devices, on_device(): normed_all = lax.all_gather(normed, 'tensor', axis=0, tiled=True)  37.2 us
    unnamed x13, local copies, waits for them, and re-layouts  30.3 us
    dot_general x1, matrix products, on_device(): jnp.dot(units, lax.all_gather(w_down, 'frame', axis=1, tiled=True), prefe...  12.2 us
  transfers between devices with their start and end apart: 21, of which 20 were waited for; matrix products, arithmetic and copies ran while one was open for 8% of the time, Pallas kernels for 0%

commit v1 on v0

--- a/solution.py
+++ b/solution.py
@@ -5,6 +5,11 @@
 from jax.sharding import PartitionSpec as P
 
 STEPS = 50
+
+
+def gather_over(block, name, along):
+    outgoing = jnp.stack([block] * lax.axis_size(name))
+    return jnp.concatenate(lax.all_to_all(outgoing, name, 0, 0), axis=along)
 
 
 def shifted(block, axis, distance):
@@ -103,11 +108,7 @@
         jnp.bfloat16
     )
     normed_all = lax.all_gather(normed, "tensor", axis=0, tiled=True)
-    up_sums = jnp.dot(
-        normed_all,
-        lax.all_gather(w_up, "frame", axis=0, tiled=True),
-        preferred_element_type=jnp.float32,
-    )
+    up_sums = jnp.dot(normed_all, gather_over(w_up, "frame", 0), preferred_element_type=jnp.float32)
     units = jax.nn.gelu(up_sums, approximate=True).astype(jnp.bfloat16)
     unit_terms = jnp.dot(
         units,

time: 476 us -> 454 us (0.954)
  waiting for transfers between devices: 318 us -> 271 us
  starting transfers between devices: 73.3 us -> 95.3 us
    all_to_all x0 -> x1, waiting for transfers between devices: none -> 81.5 us  [gather_over(): return jnp.concatenate(lax.all_to_all(outgoing, name, 0, 0), axis=along)]
    all_gather x1 -> x0, waiting for transfers between devices: 66.8 us -> none  [on_device(): lax.all_gather(w_up, 'frame', axis=0, tiled=True)]
    all_gather x1, waiting for transfers between devices: 69.5 us -> 38.8 us  [on_device(): lax.all_gather(w_down, 'frame', axis=1, tiled=True)]
    unnamed x8 -> x7, waiting for transfers between devices: 99.3 us -> 74.3 us
    all_to_all x0 -> x1, starting transfers between devices: none -> 22.1 us  [gather_over(): return jnp.concatenate(lax.all_to_all(outgoing, name, 0, 0), axis=along)]
    reshape x1 -> x2, local copies, waits for them, and re-layouts: 0.73 us -> 8.65 us  [the longest x1 7.92 us: gather_over(): return jnp.concatenate(lax.all_to_all(outgoing, name, 0, 0), axis=along)]
    unnamed x13 -> x14, local copies, waits for them, and re-layouts: 30.3 us -> 22.6 us
    all_gather x1, waiting for transfers between devices: 37.2 us -> 31.6 us  [on_device(): normed_all = lax.all_gather(normed, 'tensor', axis=0, tiled=True)]
  transfers between devices with their start and end apart: 21 -> 21, of which waited for: 20 -> 20; matrix products, arithmetic and copies ran while one was open for 8% -> 9% of each run, Pallas kernels for 0% -> 0%
where the time goes in v1:
time: 454 us; the launch traced here: 453 us
  waiting for transfers between devices  271 us (60%)
  starting transfers between devices  95.3 us (21%)
  local copies, waits for them, and re-layouts  34.4 us (8%)
  matrix products  26.2 us (6%)
  between operations  14.7 us (3%)
  other arithmetic  10.9 us (2%)
    all_to_all x1, waiting for transfers between devices, gather_over(): return jnp.concatenate(lax.all_to_all(outgoing, name, 0, 0), axis=along)  81.5 us
    unnamed x7, waiting for transfers between devices  74.3 us
    ppermute x15, starting transfers between devices, shifted(): return lax.ppermute(block, axis, route)  72.9 us
    ppermute x15, waiting for transfers between devices, shifted(): return lax.ppermute(block, axis, route)  45 us
    all_gather x1, waiting for transfers between devices, on_device(): lax.all_gather(w_down, 'frame', axis=1, tiled=True)  38.8 us
    all_gather x1, waiting for transfers between devices, on_device(): normed_all = lax.all_gather(normed, 'tensor', axis=0, tiled=True)  31.6 us
    unnamed x14, local copies, waits for them, and re-layouts  22.6 us
    all_to_all x1, starting transfers between devices, gather_over(): return jnp.concatenate(lax.all_to_all(outgoing, name, 0, 0), axis=along)  22.1 us
  transfers between devices with their start and end apart: 21, of which 20 were waited for; matrix products, arithmetic and copies ran while one was open for 9% of the time, Pallas kernels for 0%

profile of v1, /device:TPU:1, one launch (start us, length us, event | category | flops | bytes accessed | tf_op | source)
XLA Modules:
  0.0 453.0 jit_solution(14670788732547613811)
XLA Ops:
  13.8 120.2 %while.11 = (s32[]{:T(128)}, f32[5,112,112]{2,1,0:T(8,128)S(1)}, f32[5,1,1]{0,2,1:T(1,128)S(1)}, f32[5,112,112]{2,1,0:T(8,128)S(1)}, s32[]{:T(128)}, /*index=5*/s32[]{:T(128)}) while((s32[]{:T(128)}, f32[5,112,112]{2,1,0:T(8,128)S(1)}, f32[5,1,1]{0,2,1:T(1,128)S(1)}, f32[5,112,112]{2,1,0:T(8,128)S(1)}, s32[]{:T(128)}, ...), condition=%wide.region_3.4_spmd.clone, body=%wide.region_2.3_spmd.clone.sunk | while | flops 313603 | bytes 1505419 | solution.py:95
  13.9 4.4 collective-permute-start
  20.9 4.1 collective-permute-start
  25.0 3.9 collective-permute-done
  29.1 5.2 %collective-permute-start = (bf16[5,112,112]{2,1,0:T(8,128)(2,1)S(1)}, bf16[5,112,112]{2,1,0:T(8,128)(2,1)S(1)}, u32[]{:S(2)}, u32[]{:S(2)}) collective-permute-start(bf16[5,112,112]{2,1,0:T(8,128)(2,1)S(1)} %fusion.58), channel_id=1, source_target_pairs={{0,4},{4,8},{8,12},{12,16},{16,20},{20,24},{24,28},{28,32},{32,36}... | collective-permute-start | bytes 376328 | tf_op jit(solution)/shard_map/while/body/eval_jaxpr/ppermute | solution.py:18
  34.2 4.6 %collective-permute-done = bf16[5,112,112]{2,1,0:T(8,128)(2,1)S(1)} collective-permute-done((bf16[5,112,112]{2,1,0:T(8,128)(2,1)S(1)}, bf16[5,112,112]{2,1,0:T(8,128)(2,1)S(1)}, u32[]{:S(2)}, u32[]{:S(2)}) %collective-permute-start) | collective-permute-done | bytes 125472 | tf_op jit(solution)/shard_map/while/body/eval_jaxpr/ppermute | solution.py:18
  39.0 4.1 collective-permute-start
  43.1 4.7 %collective-permute-done = bf16[5,112,112]{2,1,0:T(8,128)(2,1)S(1)} collective-permute-done((bf16[5,112,112]{2,1,0:T(8,128)(2,1)S(1)}, bf16[5,112,112]{2,1,0:T(8,128)(2,1)S(1)}, u32[]{:S(2)}, u32[]{:S(2)}) %collective-permute-start) | collective-permute-done | bytes 125472 | tf_op jit(solution)/shard_map/while/body/eval_jaxpr/ppermute | solution.py:18
  48.0 4.1 collective-permute-start
  55.8 4.4 collective-permute-start
  63.9 5.8 %collective-permute-start = (bf16[5,112,112]{2,1,0:T(8,128)(2,1)S(1)}, bf16[5,112,112]{2,1,0:T(8,128)(2,1)S(1)}, u32[]{:S(2)}, u32[]{:S(2)}) collective-permute-start(bf16[5,112,112]{2,1,0:T(8,128)(2,1)S(1)} %fusion.58), channel_id=1, source_target_pairs={{0,4},{4,8},{8,12},{12,16},{16,20},{20,24},{24,28},{28,32},{32,36}... | collective-permute-start | bytes 376328 | tf_op jit(solution)/shard_map/while/body/eval_jaxpr/ppermute | solution.py:18
  73.6 5.2 %collective-permute-start = (bf16[5,112,112]{2,1,0:T(8,128)(2,1)S(1)}, bf16[5,112,112]{2,1,0:T(8,128)(2,1)S(1)}, u32[]{:S(2)}, u32[]{:S(2)}) collective-permute-start(bf16[5,112,112]{2,1,0:T(8,128)(2,1)S(1)} %fusion.58), channel_id=1, source_target_pairs={{0,4},{4,8},{8,12},{12,16},{16,20},{20,24},{24,28},{28,32},{32,36}... | collective-permute-start | bytes 376328 | tf_op jit(solution)/shard_map/while/body/eval_jaxpr/ppermute | solution.py:18
  81.2 5.2 %collective-permute-start = (bf16[5,112,112]{2,1,0:T(8,128)(2,1)S(1)}, bf16[5,112,112]{2,1,0:T(8,128)(2,1)S(1)}, u32[]{:S(2)}, u32[]{:S(2)}) collective-permute-start(bf16[5,112,112]{2,1,0:T(8,128)(2,1)S(1)} %fusion.58), channel_id=1, source_target_pairs={{0,4},{4,8},{8,12},{12,16},{16,20},{20,24},{24,28},{28,32},{32,36}... | collective-permute-start | bytes 376328 | tf_op jit(solution)/shard_map/while/body/eval_jaxpr/ppermute | solution.py:18
  88.6 4.4 collective-permute-start
  95.2 5.6 %collective-permute-start = (bf16[5,112,112]{2,1,0:T(8,128)(2,1)S(1)}, bf16[5,112,112]{2,1,0:T(8,128)(2,1)S(1)}, u32[]{:S(2)}, u32[]{:S(2)}) collective-permute-start(bf16[5,112,112]{2,1,0:T(8,128)(2,1)S(1)} %fusion.58), channel_id=1, source_target_pairs={{0,4},{4,8},{8,12},{12,16},{16,20},{20,24},{24,28},{28,32},{32,36}... | collective-permute-start | bytes 376328 | tf_op jit(solution)/shard_map/while/body/eval_jaxpr/ppermute | solution.py:18
  103.0 5.1 %collective-permute-start = (bf16[5,112,112]{2,1,0:T(8,128)(2,1)S(1)}, bf16[5,112,112]{2,1,0:T(8,128)(2,1)S(1)}, u32[]{:S(2)}, u32[]{:S(2)}) collective-permute-start(bf16[5,112,112]{2,1,0:T(8,128)(2,1)S(1)} %fusion.58), channel_id=1, source_target_pairs={{0,4},{4,8},{8,12},{12,16},{16,20},{20,24},{24,28},{28,32},{32,36}... | collective-permute-start | bytes 376328 | tf_op jit(solution)/shard_map/while/body/eval_jaxpr/ppermute | solution.py:18
  111.1 5.6 %collective-permute-start = (bf16[5,112,112]{2,1,0:T(8,128)(2,1)S(1)}, bf16[5,112,112]{2,1,0:T(8,128)(2,1)S(1)}, u32[]{:S(2)}, u32[]{:S(2)}) collective-permute-start(bf16[5,112,112]{2,1,0:T(8,128)(2,1)S(1)} %fusion.58), channel_id=1, source_target_pairs={{0,4},{4,8},{8,12},{12,16},{16,20},{20,24},{24,28},{28,32},{32,36}... | collective-permute-start | bytes 376328 | tf_op jit(solution)/shard_map/while/body/eval_jaxpr/ppermute | solution.py:18
  119.9 5.4 %collective-permute-start = (bf16[5,112,112]{2,1,0:T(8,128)(2,1)S(1)}, bf16[5,112,112]{2,1,0:T(8,128)(2,1)S(1)}, u32[]{:S(2)}, u32[]{:S(2)}) collective-permute-start(bf16[5,112,112]{2,1,0:T(8,128)(2,1)S(1)} %fusion.58), channel_id=1, source_target_pairs={{0,4},{4,8},{8,12},{12,16},{16,20},{20,24},{24,28},{28,32},{32,36}... | collective-permute-start | bytes 376328 | tf_op jit(solution)/shard_map/while/body/eval_jaxpr/ppermute | solution.py:18
  127.5 4.4 collective-permute-start
  134.7 3.9 fusion.17
  142.9 4.4 convolution_convert_fusion.1
  147.3 4.3 copy.26
  155.3 22.1 %all-to-all-start = ((bf16[16,140,1120]{2,1,0:T(8,128)(2,1)}), bf16[16,140,1120]{2,1,0:T(8,128)(2,1)}, u32[]{:S(2)}, u32[]{:S(2)}) async-start(bf16[16,140,1120]{2,1,0:T(8,128)(2,1)} %stack.2), calls=%async_computation | async-start | bytes 10616832 | tf_op jit(solution)/shard_map/all_to_all | solution.py:12
  181.3 36.1 %reduce-scatter.7.cloned.1.call-done = bf16[128,2240]{1,0:T(8,128)(2,1)} async-done(((bf16[512,2240]{1,0:T(8,128)(2,1)}), bf16[128,2240]{1,0:T(8,128)(2,1)}) %reduce-scatter.7.cloned.1.call-update) | async-done | bytes 573456
  222.0 81.5 %all-to-all-done = bf16[16,140,1120]{2,1,0:T(8,128)(2,1)} async-done(((bf16[16,140,1120]{2,1,0:T(8,128)(2,1)}), bf16[16,140,1120]{2,1,0:T(8,128)(2,1)}, u32[]{:S(2)}, u32[]{:S(2)}) %all-to-all-start) | async-done | bytes 5017632 | tf_op jit(solution)/shard_map/all_to_all | solution.py:12
  303.5 7.9 %reshape.178 = bf16[2240,1120]{1,0:T(8,128)(2,1)} reshape(bf16[16,140,1120]{2,1,0:T(8,128)(2,1)} %all-to-all-done) | data formatting | bytes 10035200 | tf_op jit(solution)/shard_map/reshape | solution.py:12
  311.4 38.8 %all-gather.10.cloned.1.call-done = bf16[16,140,1120]{2,1,0:T(8,128)(2,1)} async-done(((bf16[1,140,1120]{2,1,0:T(8,128)(2,1)}), bf16[16,140,1120]{2,1,0:T(8,128)(2,1)}) %all-gather.10.cloned.1.call-update) | async-done | bytes 5017616 | tf_op jit(solution)/shard_map/all_gather | solution.py:115
  350.2 7.9 %reshape.191 = bf16[2240,1120]{1,0:T(8,128)(2,1)} reshape(bf16[16,140,1120]{2,1,0:T(8,128)(2,1)} %all-gather.10.cloned.1.call-done) | data formatting | bytes 10035200
  358.0 31.6 %all-gather.6.cloned.1.call-done = bf16[512,2240]{0,1:T(8,128)(2,1)} async-done(((bf16[128,2240]{0,1:T(8,128)(2,1)}), bf16[512,2240]{0,1:T(8,128)(2,1)}) %all-gather.6.cloned.1.call-update) | async-done | bytes 2293776 | tf_op jit(solution)/shard_map/all_gather | solution.py:110
  389.6 12.2 %convolution_convert_fusion = bf16[512,2240]{0,1:T(8,128)(2,1)} fusion(bf16[2240,1120]{1,0:T(8,128)(2,1)} %reshape.191, bf16[512,2240]{0,1:T(8,128)(2,1)} %all-gather.6.cloned.1.call-done, bf16[2240,1120]{1,0:T(8,128)(2,1)} %reshape.178), kind=kOutput, calls=%fused_computation.4 | convolution fusion | flops 5144330240 | bytes 14622720 | tf_op jit(solution)/shard_map/dot_general | solution.py:113
  401.9 4.2 copy.28
  406.2 36.8 %reduce-scatter.9.cloned.1.call-done = bf16[128,2240]{1,0:T(8,128)(2,1)} async-done(((bf16[512,2240]{1,0:T(8,128)(2,1)}), bf16[128,2240]{1,0:T(8,128)(2,1)}) %reduce-scatter.9.cloned.1.call-update) | async-done | bytes 573456
  (93 shorter events, 60.1 us)
Async XLA Ops:
  7.2 126.8 %copy-start = (bf16[512,560]{0,1:T(8,128)(2,1)S(1)}, bf16[512,560]{0,1:T(8,128)(2,1)}, u32[]{:S(2)}) copy-start(bf16[512,560]{0,1:T(8,128)(2,1)} %param.14) | copy-start | bytes 1720324
  7.2 132.5 %all-gather.8.cloned.1.call-start = ((), (), s32[]{:S(2)}) async-start(), calls=%async_computation.4 | async-start | bytes 3133440 | tf_op jit(solution)/shard_map/all_gather | solution.py:100
  7.9 209.5 %reduce-scatter.7.cloned.1.call-start = ((), (), s32[]{:S(2)}) async-start(), calls=%async_computation.6 | async-start | bytes 2949120
  13.9 6.8 %collective-permute-start = (bf16[5,112,112]{2,1,0:T(8,128)(2,1)S(1)}, bf16[5,112,112]{2,1,0:T(8,128)(2,1)S(1)}, u32[]{:S(2)}, u32[]{:S(2)}) collective-permute-start(bf16[5,112,112]{2,1,0:T(8,128)(2,1)S(1)} %fusion.58), channel_id=1, source_target_pairs={{0,4},{4,8},{8,12},{12,16},{16,20},{20,24},{24,28},{28,32},{32,36}... | collective-permute-start | bytes 376328 | tf_op jit(solution)/shard_map/while/body/eval_jaxpr/ppermute | solution.py:18
  20.9 8.0 %collective-permute-start = (bf16[5,112,112]{2,1,0:T(8,128)(2,1)S(1)}, bf16[5,112,112]{2,1,0:T(8,128)(2,1)S(1)}, u32[]{:S(2)}, u32[]{:S(2)}) collective-permute-start(bf16[5,112,112]{2,1,0:T(8,128)(2,1)S(1)} %fusion.58), channel_id=1, source_target_pairs={{0,4},{4,8},{8,12},{12,16},{16,20},{20,24},{24,28},{28,32},{32,36}... | collective-permute-start | bytes 376328 | tf_op jit(solution)/shard_map/while/body/eval_jaxpr/ppermute | solution.py:18
  29.1 9.8 %collective-permute-start = (bf16[5,112,112]{2,1,0:T(8,128)(2,1)S(1)}, bf16[5,112,112]{2,1,0:T(8,128)(2,1)S(1)}, u32[]{:S(2)}, u32[]{:S(2)}) collective-permute-start(bf16[5,112,112]{2,1,0:T(8,128)(2,1)S(1)} %fusion.58), channel_id=1, source_target_pairs={{0,4},{4,8},{8,12},{12,16},{16,20},{20,24},{24,28},{28,32},{32,36}... | collective-permute-start | bytes 376328 | tf_op jit(solution)/shard_map/while/body/eval_jaxpr/ppermute | solution.py:18
  39.0 8.9 %collective-permute-start = (bf16[5,112,112]{2,1,0:T(8,128)(2,1)S(1)}, bf16[5,112,112]{2,1,0:T(8,128)(2,1)S(1)}, u32[]{:S(2)}, u32[]{:S(2)}) collective-permute-start(bf16[5,112,112]{2,1,0:T(8,128)(2,1)S(1)} %fusion.58), channel_id=1, source_target_pairs={{0,4},{4,8},{8,12},{12,16},{16,20},{20,24},{24,28},{28,32},{32,36}... | collective-permute-start | bytes 376328 | tf_op jit(solution)/shard_map/while/body/eval_jaxpr/ppermute | solution.py:18
  48.0 7.7 %collective-permute-start = (bf16[5,112,112]{2,1,0:T(8,128)(2,1)S(1)}, bf16[5,112,112]{2,1,0:T(8,128)(2,1)S(1)}, u32[]{:S(2)}, u32[]{:S(2)}) collective-permute-start(bf16[5,112,112]{2,1,0:T(8,128)(2,1)S(1)} %fusion.58), channel_id=1, source_target_pairs={{0,4},{4,8},{8,12},{12,16},{16,20},{20,24},{24,28},{28,32},{32,36}... | collective-permute-start | bytes 376328 | tf_op jit(solution)/shard_map/while/body/eval_jaxpr/ppermute | solution.py:18
  55.8 7.9 %collective-permute-start = (bf16[5,112,112]{2,1,0:T(8,128)(2,1)S(1)}, bf16[5,112,112]{2,1,0:T(8,128)(2,1)S(1)}, u32[]{:S(2)}, u32[]{:S(2)}) collective-permute-start(bf16[5,112,112]{2,1,0:T(8,128)(2,1)S(1)} %fusion.58), channel_id=1, source_target_pairs={{0,4},{4,8},{8,12},{12,16},{16,20},{20,24},{24,28},{28,32},{32,36}... | collective-permute-start | bytes 376328 | tf_op jit(solution)/shard_map/while/body/eval_jaxpr/ppermute | solution.py:18
  63.9 9.6 %collective-permute-start = (bf16[5,112,112]{2,1,0:T(8,128)(2,1)S(1)}, bf16[5,112,112]{2,1,0:T(8,128)(2,1)S(1)}, u32[]{:S(2)}, u32[]{:S(2)}) collective-permute-start(bf16[5,112,112]{2,1,0:T(8,128)(2,1)S(1)} %fusion.58), channel_id=1, source_target_pairs={{0,4},{4,8},{8,12},{12,16},{16,20},{20,24},{24,28},{28,32},{32,36}... | collective-permute-start | bytes 376328 | tf_op jit(solution)/shard_map/while/body/eval_jaxpr/ppermute | solution.py:18
  73.6 7.4 %collective-permute-start = (bf16[5,112,112]{2,1,0:T(8,128)(2,1)S(1)}, bf16[5,112,112]{2,1,0:T(8,128)(2,1)S(1)}, u32[]{:S(2)}, u32[]{:S(2)}) collective-permute-start(bf16[5,112,112]{2,1,0:T(8,128)(2,1)S(1)} %fusion.58), channel_id=1, source_target_pairs={{0,4},{4,8},{8,12},{12,16},{16,20},{20,24},{24,28},{28,32},{32,36}... | collective-permute-start | bytes 376328 | tf_op jit(solution)/shard_map/while/body/eval_jaxpr/ppermute | solution.py:18
  81.2 7.2 %collective-permute-start = (bf16[5,112,112]{2,1,0:T(8,128)(2,1)S(1)}, bf16[5,112,112]{2,1,0:T(8,128)(2,1)S(1)}, u32[]{:S(2)}, u32[]{:S(2)}) collective-permute-start(bf16[5,112,112]{2,1,0:T(8,128)(2,1)S(1)} %fusion.58), channel_id=1, source_target_pairs={{0,4},{4,8},{8,12},{12,16},{16,20},{20,24},{24,28},{28,32},{32,36}... | collective-permute-start | bytes 376328 | tf_op jit(solution)/shard_map/while/body/eval_jaxpr/ppermute | solution.py:18
  88.6 6.4 %collective-permute-start = (bf16[5,112,112]{2,1,0:T(8,128)(2,1)S(1)}, bf16[5,112,112]{2,1,0:T(8,128)(2,1)S(1)}, u32[]{:S(2)}, u32[]{:S(2)}) collective-permute-start(bf16[5,112,112]{2,1,0:T(8,128)(2,1)S(1)} %fusion.58), channel_id=1, source_target_pairs={{0,4},{4,8},{8,12},{12,16},{16,20},{20,24},{24,28},{28,32},{32,36}... | collective-permute-start | bytes 376328 | tf_op jit(solution)/shard_map/while/body/eval_jaxpr/ppermute | solution.py:18
  95.2 7.7 %collective-permute-start = (bf16[5,112,112]{2,1,0:T(8,128)(2,1)S(1)}, bf16[5,112,112]{2,1,0:T(8,128)(2,1)S(1)}, u32[]{:S(2)}, u32[]{:S(2)}) collective-permute-start(bf16[5,112,112]{2,1,0:T(8,128)(2,1)S(1)} %fusion.58), channel_id=1, source_target_pairs={{0,4},{4,8},{8,12},{12,16},{16,20},{20,24},{24,28},{28,32},{32,36}... | collective-permute-start | bytes 376328 | tf_op jit(solution)/shard_map/while/body/eval_jaxpr/ppermute | solution.py:18
  103.0 8.0 %collective-permute-start = (bf16[5,112,112]{2,1,0:T(8,128)(2,1)S(1)}, bf16[5,112,112]{2,1,0:T(8,128)(2,1)S(1)}, u32[]{:S(2)}, u32[]{:S(2)}) collective-permute-start(bf16[5,112,112]{2,1,0:T(8,128)(2,1)S(1)} %fusion.58), channel_id=1, source_target_pairs={{0,4},{4,8},{8,12},{12,16},{16,20},{20,24},{24,28},{28,32},{32,36}... | collective-permute-start | bytes 376328 | tf_op jit(solution)/shard_map/while/body/eval_jaxpr/ppermute | solution.py:18
  111.1 8.7 %collective-permute-start = (bf16[5,112,112]{2,1,0:T(8,128)(2,1)S(1)}, bf16[5,112,112]{2,1,0:T(8,128)(2,1)S(1)}, u32[]{:S(2)}, u32[]{:S(2)}) collective-permute-start(bf16[5,112,112]{2,1,0:T(8,128)(2,1)S(1)} %fusion.58), channel_id=1, source_target_pairs={{0,4},{4,8},{8,12},{12,16},{16,20},{20,24},{24,28},{28,32},{32,36}... | collective-permute-start | bytes 376328 | tf_op jit(solution)/shard_map/while/body/eval_jaxpr/ppermute | solution.py:18
  119.9 7.4 %collective-permute-start = (bf16[5,112,112]{2,1,0:T(8,128)(2,1)S(1)}, bf16[5,112,112]{2,1,0:T(8,128)(2,1)S(1)}, u32[]{:S(2)}, u32[]{:S(2)}) collective-permute-start(bf16[5,112,112]{2,1,0:T(8,128)(2,1)S(1)} %fusion.58), channel_id=1, source_target_pairs={{0,4},{4,8},{8,12},{12,16},{16,20},{20,24},{24,28},{28,32},{32,36}... | collective-permute-start | bytes 376328 | tf_op jit(solution)/shard_map/while/body/eval_jaxpr/ppermute | solution.py:18
  127.5 6.5 %collective-permute-start = (bf16[5,112,112]{2,1,0:T(8,128)(2,1)S(1)}, bf16[5,112,112]{2,1,0:T(8,128)(2,1)S(1)}, u32[]{:S(2)}, u32[]{:S(2)}) collective-permute-start(bf16[5,112,112]{2,1,0:T(8,128)(2,1)S(1)} %fusion.58), channel_id=1, source_target_pairs={{0,4},{4,8},{8,12},{12,16},{16,20},{20,24},{24,28},{28,32},{32,36}... | collective-permute-start | bytes 376328 | tf_op jit(solution)/shard_map/while/body/eval_jaxpr/ppermute | solution.py:18
  151.5 1.0 copy-start.2
  151.6 198.6 %all-gather.10.cloned.1.call-start = ((), (), s32[]{:S(2)}) async-start(), calls=%async_computation.5 | async-start | bytes 5640192 | tf_op jit(solution)/shard_map/all_gather | solution.py:115
  155.3 148.2 %all-to-all-start = ((bf16[16,140,1120]{2,1,0:T(8,128)(2,1)}), bf16[16,140,1120]{2,1,0:T(8,128)(2,1)}, u32[]{:S(2)}, u32[]{:S(2)}) async-start(bf16[16,140,1120]{2,1,0:T(8,128)(2,1)} %stack.2), calls=%async_computation | async-start | bytes 10616832 | tf_op jit(solution)/shard_map/all_to_all | solution.py:12
  177.4 212.2 %all-gather.6.cloned.1.call-start = ((), (), s32[]{:S(2)}) async-start(), calls=%async_computation.3 | async-start | bytes 2867200 | tf_op jit(solution)/shard_map/all_gather | solution.py:110
  181.2 37.6 %copy-start.1 = (bf16[128,2240]{0,1:T(8,128)(2,1)S(1)}, bf16[128,2240]{0,1:T(8,128)(2,1)}, u32[]{:S(2)}) copy-start(bf16[128,2240]{0,1:T(8,128)(2,1)} %param.13) | copy-start | bytes 1720324
  221.8 221.2 %reduce-scatter.9.cloned.1.call-start = ((), (), s32[]{:S(2)}) async-start(), calls=%async_computation.7 | async-start | bytes 2949120
Sparse Core Ops, SparseCore 0:
  9.8 66.7 all-gather.7
  151.7 65.7 reduce-scatter.6
  219.2 130.8 all-gather.9
  352.4 37.1 all-gather.5
  406.2 36.6 reduce-scatter.8
